TPU v7x, 1024 devices: a whole 4x4x32 slice. The times are simulated.
1024 devices in a mesh: dp: 16 (over x, y), expert: 64 (over z, core).
Axes of the slice: x: 4, y: 4, z: 32, core: 2. Of those that a mesh axis runs over, the one named last changes fastest.
Arguments:
- routing: int32 [131072, 2], P(('dp', 'expert')), may hold values from 0 to 63, all different within a row; in each aligned block of 128 rows (0 to 127, 128 to 255, ...) at most 6 rows name the same one
- gates: float32 [131072, 2], P(('dp', 'expert')), may hold values from 0.1 to 1
- hidden: bfloat16 [16, 64, 64, 6, 768], P('dp', 'expert'), may hold values from -6 to 6
- w_down: bfloat16 [64, 768, 2048], P('expert'), may hold values from -0.21875 to 0.21875
- dout: bfloat16 [131072, 2048], P(('dp', 'expert')), may hold values from -24 to 24
Outputs:
- combined: bfloat16 [131072, 2048], P(('dp', 'expert'))
- grad_gates: float32 [131072, 2], P(('dp', 'expert'))
- grad_hidden: bfloat16 [16, 64, 64, 6, 768], P('dp', 'expert')
- grad_down: float32 [64, 768, 2048], P('expert', None, 'dp')
Inputs may be any that keep to these rules, and one draw needn't show every extreme that they name: `routing`: in each aligned block of 128 rows (the rows of one device) no expert is named by more than 6 picks, and in some block an expert is named by exactly 6.
All inputs are finite; a program needn't handle non-finite values.
Results may differ from a plain program's by a relative error of at most 0.013.
Values may be sent and summed in bfloat16 or wider, within the bound.
A program may use at most 64 MiB of HBM per device.

v0:
```python
import jax
import jax.numpy as jnp
from jax import lax
from jax.sharding import PartitionSpec as P


def slot_index(routing, experts, capacity):
    flattened = routing.reshape(-1)
    onehot = (flattened[:, None] == jnp.arange(experts, dtype=jnp.int32)[None, :]).astype(jnp.int32)
    before = jnp.cumsum(onehot, axis=0) - onehot
    ranking = jnp.sum(before * onehot, axis=1)
    return flattened * capacity + ranking


def on_device(routing, gates, hidden, w_down, dout):
    experts = lax.axis_size("expert")
    capacity = hidden.shape[3]
    hidden_units = w_down.shape[1]
    model_width = w_down.shape[2]
    tok_rows = routing.shape[0]
    picks_per = routing.shape[1]
    weight = w_down[0]
    input_rows = hidden[0, 0].reshape(-1, hidden_units)
    outputs = jnp.dot(input_rows, weight, preferred_element_type=jnp.float32).astype(jnp.bfloat16)
    outputs = outputs.reshape(experts, capacity, model_width)
    returned = lax.all_to_all(outputs, "expert", split_axis=0, concat_axis=0, tiled=True)
    location = slot_index(routing, experts, capacity)
    picked = jnp.take(returned.reshape(experts * capacity, model_width), location, axis=0)
    picked = picked.reshape(tok_rows, picks_per, model_width).astype(jnp.float32)
    combined = jnp.sum(gates[..., None] * picked, axis=1).astype(jnp.bfloat16)
    grad_float = dout.astype(jnp.float32)
    grad_gates = jnp.sum(picked * grad_float[:, None, :], axis=2)
    scaled = (
        (gates[..., None] * grad_float[:, None, :]).astype(jnp.bfloat16).reshape(-1, model_width)
    )
    slot_grads = jnp.zeros((experts * capacity, model_width), jnp.bfloat16).at[location].set(scaled)
    slot_grads = slot_grads.reshape(experts, capacity, model_width)
    received = lax.all_to_all(slot_grads, "expert", split_axis=0, concat_axis=0, tiled=True)
    count_items = received.shape[1]
    flattened = received.reshape(-1, model_width)
    grad_rows = lax.dot_general(
        flattened, weight, (((1,), (1,)), ((), ())), preferred_element_type=jnp.float32
    )
    grad_hidden = grad_rows.astype(jnp.bfloat16).reshape(experts, count_items, hidden_units)
    arrived_rows = received.reshape(-1, model_width)
    partial_grad = lax.dot_general(
        input_rows, arrived_rows, (((0,), (0,)), ((), ())), preferred_element_type=jnp.float32
    )
    grad_down = lax.psum_scatter(
        partial_grad.astype(jnp.bfloat16), "dp", scatter_dimension=1, tiled=True
    ).astype(jnp.float32)
    return (combined, grad_gates, grad_hidden[None, None], grad_down[None])


def solution(mesh):
    placed = (
        P(("dp", "expert"), None),
        P(("dp", "expert"), None),
        P("dp", "expert", None, None, None),
        P("expert", None, None),
        P(("dp", "expert"), None),
    )
    return jax.shard_map(
        on_device,
        mesh=mesh,
        in_specs=placed,
        out_specs=(
            P(("dp", "expert"), None),
            P(("dp", "expert"), None),
            P("dp", "expert", None, None, None),
            P("expert", None, "dp"),
        ),
        check_vma=False,
    )
```

profile of v0, /device:TPU:6, one launch (start us, length us, event | category | flops | bytes accessed | tf_op | source)
XLA Modules:
  0.0 498.2 jit_solution(745861883193378473)
XLA Ops:
  7.2 0.0 copy-start
  7.2 0.9 copy.14
  8.1 0.1 eq.26
  8.3 0.1 reshape.102
  8.4 0.6 reduce-window.6
  9.0 0.2 slice_reduce_fusion
  9.3 0.1 mul.61
  9.4 3.5 mul.63
  12.9 0.0 copy-start.1
  12.9 3.7 mul.64
  16.5 0.0 copy-done.1
  16.5 0.1 copy.13
  16.6 0.1 mul.66
  16.8 0.1 fusion.16
  16.9 4.6 scatter_custom_fusion
  21.5 3.7 reshape.106
  25.2 29.6 %all-to-all-start.1 = ((bf16[64,6,2048]{2,1,0:T(8,128)(2,1)}), bf16[64,6,2048]{2,1,0:T(8,128)(2,1)}, u32[]{:S(2)}, u32[]{:S(2)}) async-start(bf16[64,6,2048]{2,1,0:T(8,128)(2,1)} %reshape.106), calls=%async_computation.1 | async-start | bytes 4194304 | tf_op jit(solution)/shard_map/all_to_all | solution.py:38
  54.9 2.3 copy.18
  57.2 2.1 reshape_squeeze.3
  59.2 0.0 copy-done
  59.2 3.6 fusion.5
  62.9 3.7 reshape.104
  66.5 188.7 %all-to-all-done.1 = bf16[64,6,2048]{2,1,0:T(8,128)(2,1)} async-done(((bf16[64,6,2048]{2,1,0:T(8,128)(2,1)}), bf16[64,6,2048]{2,1,0:T(8,128)(2,1)}, u32[]{:S(2)}, u32[]{:S(2)}) %all-to-all-start.1) | async-done | bytes 1572896 | tf_op jit(solution)/shard_map/all_to_all | solution.py:38
  255.3 5.6 %all-to-all-start = ((bf16[64,6,2048]{2,1,0:T(8,128)(2,1)}), bf16[64,6,2048]{2,1,0:T(8,128)(2,1)}, u32[]{:S(2)}, u32[]{:S(2)}) async-start(bf16[64,6,2048]{2,1,0:T(8,128)(2,1)} %reshape.104), calls=%async_computation | async-start | bytes 4194304 | tf_op jit(solution)/shard_map/all_to_all | solution.py:26
  260.8 0.2 reduce-scatter.2.cloned.1.call-start
  261.1 3.8 reshape.107
  264.8 5.0 %fusion.4 = bf16[768,2048]{0,1:T(8,128)(2,1)} fusion(bf16[384,2048]{1,0:T(8,128)(2,1)} %reshape.107, bf16[384,768]{1,0:T(8,128)(2,1)} %reshape_squeeze.3), kind=kOutput, calls=%fused_computation.7 | convolution fusion | flops 1209532416 | bytes 5308416 | tf_op jit(solution)/shard_map/dot_general | solution.py:46
  269.9 0.0 reduce-scatter.2.cloned.1.call-update
  269.9 0.1 reduce_sum.34
  270.1 0.1 broadcast_in_dim.33
  270.2 191.0 %all-to-all-done = bf16[64,6,2048]{2,1,0:T(8,128)(2,1)} async-done(((bf16[64,6,2048]{2,1,0:T(8,128)(2,1)}), bf16[64,6,2048]{2,1,0:T(8,128)(2,1)}, u32[]{:S(2)}, u32[]{:S(2)}) %all-to-all-start) | async-done | bytes 1572896 | tf_op jit(solution)/shard_map/all_to_all | solution.py:26
  461.2 3.7 reshape.105
  465.0 4.9 gather_fusion
  469.9 2.5 gather.7
  472.4 2.3 multiply_reduce_fusion
  474.7 0.1 reduce_sum.38
  474.9 0.6 copy.20
  475.5 3.6 fusion.8
  479.2 2.1 broadcast_in_dim_reshape.4
  481.2 2.0 copy.21
  483.3 6.2 %multiply_reduce_fusion.1 = bf16[128,2048]{1,0:T(8,128)(2,1)} fusion(bf16[128,2,2048]{2,1,0:T(2,128)(2,1)} %gather.7, pred[128,2]{1,0:T(8,128)(4,1)S(1)} %compare_and_fusion, f32[128,2]{1,0:T(8,128)S(1)} %copy.13), kind=kLoop, calls=%fused_computation.11 | loop fusion | flops 1835008 | bytes 1574144 | tf_op jit(solution)/shard_map/reduce_sum | solution.py:30
  489.5 0.0 reduce-scatter.2.cloned.1.call-done
  489.5 1.0 bitcast_convert_fusion
  490.5 0.9 copy.22
  (7 shorter events, 0.1 us)
Async XLA Ops:
  7.2 52.1 %copy-start = (bf16[1,768,2048]{2,1,0:T(8,128)(2,1)S(1)}, bf16[1,768,2048]{2,1,0:T(8,128)(2,1)}, u32[]{:S(2)}) copy-start(bf16[1,768,2048]{2,1,0:T(8,128)(2,1)} %param.8) | copy-start | bytes 9437188
  12.9 3.7 copy-start.1
  25.2 230.0 %all-to-all-start.1 = ((bf16[64,6,2048]{2,1,0:T(8,128)(2,1)}), bf16[64,6,2048]{2,1,0:T(8,128)(2,1)}, u32[]{:S(2)}, u32[]{:S(2)}) async-start(bf16[64,6,2048]{2,1,0:T(8,128)(2,1)} %reshape.106), calls=%async_computation.1 | async-start | bytes 4194304 | tf_op jit(solution)/shard_map/all_to_all | solution.py:38
  255.3 206.0 %all-to-all-start = ((bf16[64,6,2048]{2,1,0:T(8,128)(2,1)}), bf16[64,6,2048]{2,1,0:T(8,128)(2,1)}, u32[]{:S(2)}, u32[]{:S(2)}) async-start(bf16[64,6,2048]{2,1,0:T(8,128)(2,1)} %reshape.104), calls=%async_computation | async-start | bytes 4194304 | tf_op jit(solution)/shard_map/all_to_all | solution.py:26
  260.8 228.7 %reduce-scatter.2.cloned.1.call-start = ((), (), s32[]{:S(2)}) async-start(), calls=%async_computation.3 | async-start | bytes 3342336 | tf_op jit(solution)/shard_map/reduce_scatter | solution.py:49
Sparse Core Ops, SparseCore 0:
  270.0 112.8 reduce-scatter.1
where the time goes:
time: 499 us; the launch traced here: 498 us
  waiting for transfers between devices  380 us (76%)
  local copies, waits for them, and re-layouts  41.8 us (8%)
  starting transfers between devices  35.4 us (7%)
  other arithmetic  14.9 us (3%)
  between operations  14.1 us (3%)
  matrix products  12.3 us (2%)
    all_to_all x1, waiting for transfers between devices, on_device(): lax.all_to_all(outputs, 'expert', split_axis=0, concat_axis=0, tiled=True)  191 us
    all_to_all x1, waiting for transfers between devices, on_device(): lax.all_to_all(slot_grads, 'expert', split_axis=0, concat_axis=0, tiled=T...  189 us
    all_to_all x1, starting transfers between devices, on_device(): lax.all_to_all(slot_grads, 'expert', split_axis=0, concat_axis=0, tiled=T...  29.6 us
  transfers between devices with their start and end apart: 3, of which 2 were waited for; matrix products, arithmetic and copies ran while one was open for 10% of the time, Pallas kernels for 0%

commit v1 on v0

v1 whole, which is shorter than its diff:
```python
import functools

import jax
import jax.numpy as jnp
from jax import lax
from jax.experimental import pallas as pl
from jax.experimental.pallas import tpu as pltpu
from jax.sharding import PartitionSpec as P

MESH = pl.DeviceIdType.MESH
F32 = jnp.float32
BF16 = jnp.bfloat16
PIECES = 8


def dot(a, b, contract):
    return lax.dot_general(a, b, ((contract[:1], contract[1:]), ((), ())), preferred_element_type=F32)


def perm(group, cap, shape_of, transposed):
    n = group * PIECES * cap
    row = lax.broadcasted_iota(jnp.int32, (n, n), 0)
    col = lax.broadcasted_iota(jnp.int32, (n, n), 1)
    if transposed:
        row, col = col, row
    line = row // group
    want = (row - line * group) * (PIECES * cap) + line
    return jnp.where(col == want, 1.0, 0.0).astype(BF16)


def to_blocks(matrix_t, rows_ref, blocks_ref, experts, cap, group):
    width = rows_ref.shape[1] // PIECES
    for g in range(experts // group):
        parts = []
        for j in range(PIECES):
            for r in range(cap):
                parts.append(rows_ref[r * experts + g * group:r * experts + (g + 1) * group, j * width:(j + 1) * width])
        stacked = jnp.concatenate(parts, axis=0)
        out = dot(matrix_t, stacked, (1, 0)).astype(BF16)
        blocks_ref[g * group:(g + 1) * group] = out.reshape(group, PIECES * cap, width)


def from_blocks(matrix, blocks_ref, rows_ref, experts, cap, group):
    width = rows_ref.shape[1] // PIECES
    for g in range(experts // group):
        stacked = blocks_ref[g * group:(g + 1) * group].reshape(group * PIECES * cap, width)
        out = dot(matrix, stacked, (1, 0)).astype(BF16)
        for j in range(PIECES):
            for r in range(cap):
                at = (j * cap + r) * group
                rows_ref[r * experts + g * group:r * experts + (g + 1) * group, j * width:(j + 1) * width] = out[at:at + group]


def column(row, n):
    a = lax.broadcasted_iota(jnp.int32, (n, n), 0)
    b = lax.broadcasted_iota(jnp.int32, (n, n), 1)
    return jnp.sum(jnp.where(a == b, row, jnp.zeros_like(row)), axis=1, keepdims=True)


def as_row(col, n):
    a = lax.broadcasted_iota(jnp.int32, (n, n), 0)
    b = lax.broadcasted_iota(jnp.int32, (n, n), 1)
    return jnp.sum(jnp.where(a == b, col, jnp.zeros_like(col)), axis=0, keepdims=True)


def before_kernel(experts, cap, group, routing_ref, gates_ref, dout_ref, blocks_ref, loc_ref, scaled, rows):
    top, tokens = routing_ref.shape
    number = lax.broadcasted_iota(jnp.int32, (experts, tokens), 0)
    hot = [number == routing_ref[k:k + 1, :] for k in range(top)]
    count = sum(jnp.where(h, 1.0, 0.0) for h in hot).astype(BF16)
    a = lax.broadcasted_iota(jnp.int32, (tokens, tokens), 0)
    b = lax.broadcasted_iota(jnp.int32, (tokens, tokens), 1)
    earlier = jnp.where(a < b, 1.0, 0.0).astype(BF16)
    before = dot(count, earlier, (1, 0))
    line = lax.broadcasted_iota(jnp.int32, (experts * cap, tokens), 0)
    onehot = []
    for k in range(top):
        rank = jnp.sum(jnp.where(hot[k], before, 0.0), axis=0, keepdims=True).astype(jnp.int32)
        loc = rank * experts + routing_ref[k:k + 1, :]
        loc_ref[k:k + 1, :] = loc
        onehot.append(jnp.where(line == loc, 1.0, 0.0).astype(BF16))
        scaled[k * tokens:(k + 1) * tokens, :] = (column(gates_ref[k:k + 1, :], tokens) * dout_ref[...].astype(F32)).astype(BF16)
    rows[...] = dot(jnp.concatenate(onehot, axis=1), scaled[...], (1, 0)).astype(BF16)
    to_blocks(perm(group, cap, None, True), rows, blocks_ref, experts, cap, group)


def after_kernel(experts, cap, group, blocks_ref, loc_ref, gates_ref, dout_ref, combined_ref, gg_ref, rows):
    top, tokens = loc_ref.shape
    from_blocks(perm(group, cap, None, False), blocks_ref, rows, experts, cap, group)
    place = lax.broadcasted_iota(jnp.int32, (tokens, experts * cap), 1)
    total = None
    grad = dout_ref[...].astype(F32)
    for k in range(top):
        onehot = jnp.where(place == column(loc_ref[k:k + 1, :], tokens), 1.0, 0.0).astype(BF16)
        picked = dot(onehot, rows[...], (1, 0))
        term = column(gates_ref[k:k + 1, :], tokens) * picked
        total = term if total is None else total + term
        gg_ref[k:k + 1, :] = as_row(jnp.sum(picked * grad, axis=1, keepdims=True), tokens)
    combined_ref[...] = total.astype(BF16)


def plan_of(half):
    groups = [[half]]
    top = half - 1
    while top >= 1:
        low = max(1, ((top - 1) // 4) * 4 + 1)
        groups.append(list(range(low, top + 1)))
        top = low - 1
    offset, total = {}, 0
    for d in range(1, half - 1):
        offset[d] = total
        total += half - 1 - d
    return groups, offset, max(total, 1)


def exchange_kernel(chips, groups_dp, cap, group, lead, at, a_ref, h_any, w_any, fb_ref, gh_ref, gd_ref,
                    a_in, h, w, sb, fa, rows, part, inbox, ring, ringh, rsem, ssem, fsem, psem, gsem, lsem):
    experts = 2 * chips
    half = chips // 2
    plan, offset, total = plan_of(half)
    me = lax.axis_index("expert")
    dp = lax.axis_index("dp")
    z = me // 2
    c = lax.rem(me, 2)
    other = 1 - c
    cols = fa.shape[2]
    hc = cols // 2

    loads = [pltpu.make_async_copy(s, d, lsem.at[i]) for i, (s, d) in enumerate(((a_ref, a_in), (h_any, h), (w_any, w)))]
    for load in loads:
        load.start()

    def chip(delta):
        return lax.rem(z + delta + chips, chips)

    barrier = pltpu.get_barrier_semaphore()
    near = [2 * chip(1) + c, 2 * chip(1) + other, 2 * chip(-1) + c, 2 * chip(-1) + other, 2 * z + other]
    for device in near:
        pl.semaphore_signal(barrier, inc=1, device_id={"expert": device}, device_id_type=MESH)
    for q in range(groups_dp - 1):
        pl.semaphore_signal(barrier, inc=1, device_id={"dp": lax.rem(dp + q + 1, groups_dp)}, device_id_type=MESH)
    loads[0].wait()
    pl.semaphore_wait(barrier, len(near) + groups_dp - 1)

    sources = (a_in, sb)
    finals = (fa, fb_ref)

    def remote(src, dst, send, recv, device):
        return pltpu.make_async_remote_copy(src_ref=src, dst_ref=dst, send_sem=send, recv_sem=recv, device_id=device, device_id_type=MESH)

    def sign(way):
        return 1 if way == 0 else -1

    def neighbour(way):
        return {"expert": 2 * chip(sign(way)) + c}

    def columns(way):
        return pl.ds(way * hc, hc)

    def final(s, way, d, src_of, is_half):
        origin = 2 * lax.rem(z - sign(way) * (d - 1) + chips, chips) + c
        dst = finals[s].at[origin, :, columns(way)] if is_half else finals[s].at[origin]
        for core in (c, other):
            remote(src_of(core), dst, ssem.at[s, way, 2], fsem.at[s], {"expert": 2 * chip(sign(way)) + core}).start()

    def hop_one(s):
        for g, ks in enumerate(plan):
            for k in reversed(ks):
                for way in (0, 1):
                    to = 2 * chip(sign(way) * k)
                    if k == half:
                        remote(sources[s].at[pl.ds(to, 2), :, columns(way)], ringh.at[s, way, pl.ds(0, 2)], ssem.at[s, way, 1],
                               rsem.at[s, way, 1, g], neighbour(way)).start()
                    elif k > 1:
                        i = offset[1] + k - 2
                        remote(sources[s].at[pl.ds(to, 2)], ring.at[s, way, pl.ds(2 * i, 2)], ssem.at[s, way, 0],
                               rsem.at[s, way, 1, g], neighbour(way)).start()
                    else:
                        final(s, way, 1, lambda core: sources[s].at[to + core], False)
        remote(sources[s].at[2 * z + other], finals[s].at[me], ssem.at[s, 0, 2], fsem.at[s], {"expert": 2 * z + other}).start()

    def hop(s, d):
        for g, ks in enumerate(plan):
            if ks[-1] < d:
                continue
            for way in (0, 1):
                if ks[-1] == half:
                    held = ringh.at[s, way, pl.ds(2 * (d - 2), 2)]
                    remote(held, held, ssem.at[s, way, 1], rsem.at[s, way, d - 1, g], neighbour(way)).wait_recv()
                    if d < half:
                        remote(held, ringh.at[s, way, pl.ds(2 * (d - 1), 2)], ssem.at[s, way, 1], rsem.at[s, way, d, g], neighbour(way)).start()
                    else:
                        final(s, way, d, lambda core: ringh.at[s, way, 2 * (d - 2) + core], True)
                    continue
                low = max(ks[0], d)
                first = offset[d - 1] + low - d
                held = ring.at[s, way, pl.ds(2 * first, 2 * (ks[-1] - low + 1))]
                remote(held, held, ssem.at[s, way, 0], rsem.at[s, way, d - 1, g], neighbour(way)).wait_recv()
                onward = max(ks[0], d + 1)
                if onward <= ks[-1]:
                    size = 2 * (ks[-1] - onward + 1)
                    remote(ring.at[s, way, pl.ds(2 * (offset[d - 1] + onward - d), size)],
                           ring.at[s, way, pl.ds(2 * (offset[d] + onward - d - 1), size)],
                           ssem.at[s, way, 0], rsem.at[s, way, d, g], neighbour(way)).start()
                if low == d:
                    final(s, way, d, lambda core: ring.at[s, way, 2 * first + core], False)

    def arrived(s):
        remote(finals[s].at[pl.ds(0, experts - 1)], finals[s].at[pl.ds(0, experts - 1)], ssem.at[s, 0, 2], fsem.at[s], neighbour(0)).wait_recv()

    def forward():
        loads[1].wait()
        loads[2].wait()
        width = w.shape[1] // 4
        for i in range(4):
            rows[:, i * width:(i + 1) * width] = dot(h[...], w[:, i * width:(i + 1) * width], (1, 0)).astype(BF16)
        to_blocks(perm(group, cap, None, True), rows, sb, experts, cap, group)
        fb_ref[me] = sb[me]

    def unpack():
        arrived(0)
        fa[me] = a_in[me]
        from_blocks(perm(group, cap, None, False), fa, rows, experts, cap, group)

    def hidden_grads():
        gh_ref[...] = dot(rows[...], w[...], (1, 1)).astype(BF16)

    def weight_grads():
        piece = part.shape[2]
        for i in range(groups_dp // 2):
            both = dot(h[...], rows[:, 2 * i * piece:2 * (i + 1) * piece], (0, 0)).astype(BF16)
            part[2 * i] = both[:, :piece]
            part[2 * i + 1] = both[:, piece:]
        for q in range(groups_dp - 1):
            to = lax.rem(dp + q + 1, groups_dp)
            remote(part.at[to], inbox.at[q], psem, gsem, {"dp": to}).start()

    work = {at: unpack, at + 1: hidden_grads, at + 2: weight_grads}
    hop_one(0)
    forward()
    for d in range(2, lead + 1):
        hop(0, d)
    hop_one(1)
    for i in range(2, half + 1):
        if lead + i - 1 <= half:
            hop(0, lead + i - 1)
        hop(1, i)
        if i in work:
            work.pop(i)()
    for job in work.values():
        job()

    remote(inbox, inbox, psem, gsem, {"dp": dp}).wait_recv()
    total_grad = part[dp].astype(F32)
    for q in range(groups_dp - 1):
        total_grad = total_grad + inbox[q].astype(F32)
    gd_ref[...] = total_grad
    arrived(1)
    for s in (0, 1):
        for way in (0, 1):
            if half > 2:
                remote(ring.at[s, way], ring.at[s, way], ssem.at[s, way, 0], rsem.at[s, way, 1, 0], neighbour(way)).wait_send()
            remote(ringh.at[s, way], ringh.at[s, way], ssem.at[s, way, 1], rsem.at[s, way, 1, 0], neighbour(way)).wait_send()
            sent = finals[s].at[pl.ds(0, 2 * (half - 1) + 1 + (1 if way == 0 else 0))]
            remote(sent, sent, ssem.at[s, way, 2], fsem.at[s], neighbour(way)).wait_send()
    remote(inbox, inbox, psem, gsem, {"dp": dp}).wait_send()


def on_device(chips, groups_dp, lead, at, routing, gates, hidden, w_down, dout):
    experts = 2 * chips
    cap, units = hidden.shape[3], hidden.shape[4]
    width = w_down.shape[2]
    tokens, top = routing.shape
    group = min(16, experts)
    cols = width // PIECES
    block = (experts, PIECES * cap, cols)
    routing_t, gates_t = routing.T, gates.T
    h = jnp.transpose(hidden[0, 0], (1, 0, 2)).reshape(cap * experts, units)
    vmem = pl.BlockSpec(memory_space=pltpu.VMEM)
    anywhere = pl.BlockSpec(memory_space=pl.ANY)

    blocks, loc = pl.pallas_call(
        functools.partial(before_kernel, experts, cap, group),
        out_shape=(jax.ShapeDtypeStruct(block, BF16), jax.ShapeDtypeStruct((top, tokens), jnp.int32)),
        in_specs=[vmem] * 3,
        out_specs=(vmem, vmem),
        scratch_shapes=[pltpu.VMEM((top * tokens, width), BF16), pltpu.VMEM((experts * cap, width), BF16)],
        name="pack",
    )(routing_t, gates_t, dout)

    half = chips // 2
    plan, _, total = plan_of(half)
    piece = width // groups_dp
    back, grad_hidden, grad_down = pl.pallas_call(
        functools.partial(exchange_kernel, chips, groups_dp, cap, group, lead, at),
        out_shape=(jax.ShapeDtypeStruct(block, BF16), jax.ShapeDtypeStruct((cap * experts, units), BF16),
                   jax.ShapeDtypeStruct((units, piece), F32)),
        in_specs=[anywhere] * 3,
        out_specs=(vmem, vmem, vmem),
        scratch_shapes=[
            pltpu.VMEM(block, BF16),
            pltpu.VMEM((cap * experts, units), BF16),
            pltpu.VMEM((units, width), BF16),
            pltpu.VMEM(block, BF16),
            pltpu.VMEM(block, BF16),
            pltpu.VMEM((cap * experts, width), BF16),
            pltpu.VMEM((groups_dp, units, piece), BF16),
            pltpu.VMEM((groups_dp - 1, units, piece), BF16),
            pltpu.VMEM((2, 2, 2 * total, PIECES * cap, cols), BF16),
            pltpu.VMEM((2, 2, 2 * (half - 1), PIECES * cap, cols // 2), BF16),
            pltpu.SemaphoreType.DMA((2, 2, half, len(plan))),
            pltpu.SemaphoreType.DMA((2, 2, 3)),
            pltpu.SemaphoreType.DMA((2,)),
            pltpu.SemaphoreType.DMA,
            pltpu.SemaphoreType.DMA,
            pltpu.SemaphoreType.DMA((3,)),
        ],
        compiler_params=pltpu.CompilerParams(collective_id=0, has_side_effects=True, vmem_limit_bytes=62 * 1024 * 1024),
        name="exchange",
    )(blocks, h, w_down[0])

    combined, grad_gates = pl.pallas_call(
        functools.partial(after_kernel, experts, cap, group),
        out_shape=(jax.ShapeDtypeStruct((tokens, width), BF16), jax.ShapeDtypeStruct((top, tokens), F32)),
        in_specs=[vmem] * 4,
        out_specs=(vmem, vmem),
        scratch_shapes=[pltpu.VMEM((experts * cap, width), BF16)],
        name="combine",
    )(back, loc, gates_t, dout)
    grad_hidden = jnp.transpose(grad_hidden.reshape(cap, experts, units), (1, 0, 2))
    return combined, grad_gates.T, grad_hidden[None, None], grad_down[None]


def solution(mesh):
    chips, groups_dp = mesh.shape["expert"] // 2, mesh.shape["dp"]
    half = chips // 2
    lead = max(1, half - 4)
    at = half - lead + 4
    placed = (
        P(("dp", "expert"), None),
        P(("dp", "expert"), None),
        P("dp", "expert", None, None, None),
        P("expert", None, None),
        P(("dp", "expert"), None),
    )
    return jax.shard_map(
        functools.partial(on_device, chips, groups_dp, lead, at),
        mesh=mesh,
        in_specs=placed,
        out_specs=(
            P(("dp", "expert"), None),
            P(("dp", "expert"), None),
            P("dp", "expert", None, None, None),
            P("expert", None, "dp"),
        ),
        check_vma=False,
    )
```

time: 499 us -> 338 us (0.68)
  the two profiles are of different devices: /device:TPU:6 before, /device:TPU:28 now
where the time goes in v1:
time: 338 us
  Pallas kernels  336 us (99%)
    pallas_call x1, Pallas kernels, on_device(): pl.pallas_call(functools.partial(exchange_kernel, chips, groups_dp, cap,...  327 us

profile of v1, /device:TPU:28, one launch (start us, length us, event | category | flops | bytes accessed | tf_op | source)
XLA Modules:
  0.0 338.0 jit_solution(2373703270080146331)
XLA Ops:
  0.6 4.2 %pack.1 = (bf16[64,48,256]{2,1,0:T(8,128)(2,1)}, s32[2,128]{1,0:T(2,128)}) custom-call(s32[2,128]{1,0:T(2,128)} %bitcast.21, f32[2,128]{1,0:T(2,128)} %bitcast.19, bf16[128,2048]{1,0:T(8,128)(2,1)} %dout_ref.3), custom_call_target="tpu_custom_call" | custom-call | tf_op jit(solution)/shard_map/pack/pallas_call | solution.py:282
  4.8 327.1 %exchange.1 = (bf16[64,48,256]{2,1,0:T(8,128)(2,1)}, bf16[384,768]{1,0:T(8,128)(2,1)}, f32[768,128]{1,0:T(8,128)}) custom-call(bf16[64,48,256]{2,1,0:T(8,128)(2,1)} %get-tuple-element.11.a_ref, bf16[384,768]{1,0:T(8,128)(2,1)} %bitcast.17, bf16[768,2048]{1,0:T(8,128)(2,1)} %bitcast.15), custom_call_target="tpu_custom_call" | custom-call | tf_op jit(solution)/shard_map/exchange/pallas_call | solution.py:294
  331.9 0.0 copy-start
  331.9 0.0 copy-start.1
  331.9 4.5 %combine.1 = (bf16[128,2048]{1,0:T(8,128)(2,1)}, f32[2,128]{1,0:T(2,128)}) custom-call(bf16[64,48,256]{2,1,0:T(8,128)(2,1)} %get-tuple-element.12.blocks_ref, s32[2,128]{1,0:T(2,128)} %get-tuple-element.13.loc_ref, f32[2,128]{1,0:T(2,128)} %bitcast.20, bf16[128,2048]{1,0:T(8,128)(2,1)} %dout_ref.3), custom_call_target="tpu_custom_call" | custom-call | tf_op jit(solution)/shard_map/combine/pallas_call | solution.py:322
  336.4 0.0 copy-done
  336.4 0.8 copy.11
  337.3 0.0 copy-done.1
  337.3 0.7 copy.12
Async XLA Ops:
  331.9 4.5 %copy-start = (bf16[384,768]{1,0:T(8,128)(2,1)S(1)}, bf16[384,768]{1,0:T(8,128)(2,1)}, u32[]{:S(2)}) copy-start(bf16[384,768]{1,0:T(8,128)(2,1)} %get-tuple-element.16) | copy-start | bytes 1769476
  331.9 5.3 %copy-start.1 = (f32[768,128]{1,0:T(8,128)S(1)}, f32[768,128]{1,0:T(8,128)}, u32[]{:S(2)}) copy-start(f32[768,128]{1,0:T(8,128)} %get-tuple-element.17) | copy-start | bytes 1179652

commit v2 on v1

--- a/solution.py
+++ b/solution.py
@@ -113,8 +113,8 @@
     return groups, offset, max(total, 1)
 
 
-def exchange_kernel(chips, groups_dp, cap, group, lead, at, a_ref, h_any, w_any, fb_ref, gh_ref, gd_ref,
-                    a_in, h, w, sb, fa, rows, part, inbox, ring, ringh, rsem, ssem, fsem, psem, gsem, lsem):
+def exchange_kernel(chips, groups_dp, cap, group, lead, a_ref, h_any, w_any, fb_ref, gh_ref, gd_ref,
+                    a_in, h, ht, w, sb, fa, rows, part, inbox, ring, ringh, rsem, ssem, fsem, psem, gsem, lsem):
     experts = 2 * chips
     half = chips // 2
     plan, offset, total = plan_of(half)
@@ -163,47 +163,45 @@
         for core in (c, other):
             remote(src_of(core), dst, ssem.at[s, way, 2], fsem.at[s], {"expert": 2 * chip(sign(way)) + core}).start()
 
-    def hop_one(s):
-        for g, ks in enumerate(plan):
-            for k in reversed(ks):
-                for way in (0, 1):
-                    to = 2 * chip(sign(way) * k)
-                    if k == half:
-                        remote(sources[s].at[pl.ds(to, 2), :, columns(way)], ringh.at[s, way, pl.ds(0, 2)], ssem.at[s, way, 1],
-                               rsem.at[s, way, 1, g], neighbour(way)).start()
-                    elif k > 1:
-                        i = offset[1] + k - 2
-                        remote(sources[s].at[pl.ds(to, 2)], ring.at[s, way, pl.ds(2 * i, 2)], ssem.at[s, way, 0],
-                               rsem.at[s, way, 1, g], neighbour(way)).start()
-                    else:
-                        final(s, way, 1, lambda core: sources[s].at[to + core], False)
-        remote(sources[s].at[2 * z + other], finals[s].at[me], ssem.at[s, 0, 2], fsem.at[s], {"expert": 2 * z + other}).start()
-
-    def hop(s, d):
-        for g, ks in enumerate(plan):
-            if ks[-1] < d:
+    def begin(s, g):
+        for k in reversed(plan[g]):
+            for way in (0, 1):
+                to = 2 * chip(sign(way) * k)
+                if k == half:
+                    remote(sources[s].at[pl.ds(to, 2), :, columns(way)], ringh.at[s, way, pl.ds(0, 2)], ssem.at[s, way, 1],
+                           rsem.at[s, way, 1, g], neighbour(way)).start()
+                elif k > 1:
+                    i = offset[1] + k - 2
+                    remote(sources[s].at[pl.ds(to, 2)], ring.at[s, way, pl.ds(2 * i, 2)], ssem.at[s, way, 0],
+                           rsem.at[s, way, 1, g], neighbour(way)).start()
+                else:
+                    final(s, way, 1, lambda core: sources[s].at[to + core], False)
+        if plan[g][0] == 1:
+            remote(sources[s].at[2 * z + other], finals[s].at[me], ssem.at[s, 0, 2], fsem.at[s], {"expert": 2 * z + other}).start()
+
+    def onward(s, g, d):
+        ks = plan[g]
+        for way in (0, 1):
+            if ks[-1] == half:
+                held = ringh.at[s, way, pl.ds(2 * (d - 2), 2)]
+                remote(held, held, ssem.at[s, way, 1], rsem.at[s, way, d - 1, g], neighbour(way)).wait_recv()
+                if d < half:
+                    remote(held, ringh.at[s, way, pl.ds(2 * (d - 1), 2)], ssem.at[s, way, 1], rsem.at[s, way, d, g], neighbour(way)).start()
+                else:
+                    final(s, way, d, lambda core: ringh.at[s, way, 2 * (d - 2) + core], True)
                 continue
-            for way in (0, 1):
-                if ks[-1] == half:
-                    held = ringh.at[s, way, pl.ds(2 * (d - 2), 2)]
-                    remote(held, held, ssem.at[s, way, 1], rsem.at[s, way, d - 1, g], neighbour(way)).wait_recv()
-                    if d < half:
-                        remote(held, ringh.at[s, way, pl.ds(2 * (d - 1), 2)], ssem.at[s, way, 1], rsem.at[s, way, d, g], neighbour(way)).start()
-                    else:
-                        final(s, way, d, lambda core: ringh.at[s, way, 2 * (d - 2) + core], True)
-                    continue
-                low = max(ks[0], d)
-                first = offset[d - 1] + low - d
-                held = ring.at[s, way, pl.ds(2 * first, 2 * (ks[-1] - low + 1))]
-                remote(held, held, ssem.at[s, way, 0], rsem.at[s, way, d - 1, g], neighbour(way)).wait_recv()
-                onward = max(ks[0], d + 1)
-                if onward <= ks[-1]:
-                    size = 2 * (ks[-1] - onward + 1)
-                    remote(ring.at[s, way, pl.ds(2 * (offset[d - 1] + onward - d), size)],
-                           ring.at[s, way, pl.ds(2 * (offset[d] + onward - d - 1), size)],
-                           ssem.at[s, way, 0], rsem.at[s, way, d, g], neighbour(way)).start()
-                if low == d:
-                    final(s, way, d, lambda core: ring.at[s, way, 2 * first + core], False)
+            low = max(ks[0], d)
+            first = offset[d - 1] + low - d
+            held = ring.at[s, way, pl.ds(2 * first, 2 * (ks[-1] - low + 1))]
+            remote(held, held, ssem.at[s, way, 0], rsem.at[s, way, d - 1, g], neighbour(way)).wait_recv()
+            rest = max(ks[0], d + 1)
+            if rest <= ks[-1]:
+                size = 2 * (ks[-1] - rest + 1)
+                remote(ring.at[s, way, pl.ds(2 * (offset[d - 1] + rest - d), size)],
+                       ring.at[s, way, pl.ds(2 * (offset[d] + rest - d - 1), size)],
+                       ssem.at[s, way, 0], rsem.at[s, way, d, g], neighbour(way)).start()
+            if low == d:
+                final(s, way, d, lambda core: ring.at[s, way, 2 * first + core], False)
 
     def arrived(s):
         remote(finals[s].at[pl.ds(0, experts - 1)], finals[s].at[pl.ds(0, experts - 1)], ssem.at[s, 0, 2], fsem.at[s], neighbour(0)).wait_recv()
@@ -217,6 +215,9 @@
         to_blocks(perm(group, cap, None, True), rows, sb, experts, cap, group)
         fb_ref[me] = sb[me]
 
+    def flip():
+        ht[...] = h[...].T
+
     def unpack():
         arrived(0)
         fa[me] = a_in[me]
@@ -225,28 +226,33 @@
     def hidden_grads():
         gh_ref[...] = dot(rows[...], w[...], (1, 1)).astype(BF16)
 
-    def weight_grads():
-        piece = part.shape[2]
+    def weight_grads(step):
+        piece, size = part.shape[2], part.shape[1] // 2
+        lines = pl.ds(step * size, size)
         for i in range(groups_dp // 2):
-            both = dot(h[...], rows[:, 2 * i * piece:2 * (i + 1) * piece], (0, 0)).astype(BF16)
-            part[2 * i] = both[:, :piece]
-            part[2 * i + 1] = both[:, piece:]
+            both = dot(ht[lines, :], rows[:, 2 * i * piece:2 * (i + 1) * piece], (1, 0)).astype(BF16)
+            part[2 * i, lines, :] = both[:, :piece]
+            part[2 * i + 1, lines, :] = both[:, piece:]
         for q in range(groups_dp - 1):
             to = lax.rem(dp + q + 1, groups_dp)
-            remote(part.at[to], inbox.at[q], psem, gsem, {"dp": to}).start()
-
-    work = {at: unpack, at + 1: hidden_grads, at + 2: weight_grads}
-    hop_one(0)
-    forward()
-    for d in range(2, lead + 1):
-        hop(0, d)
-    hop_one(1)
-    for i in range(2, half + 1):
-        if lead + i - 1 <= half:
-            hop(0, lead + i - 1)
-        hop(1, i)
-        if i in work:
-            work.pop(i)()
+            remote(part.at[to, lines, :], inbox.at[q, lines, :], psem, gsem, {"dp": to}).start()
+
+    def grads():
+        unpack()
+        weight_grads(0)
+        weight_grads(1)
+
+    work = {(1, len(plan) - 1): forward, (3, len(plan) - 1): flip, (half + 1, min(1, len(plan) - 2)): grads, (half + 2, 1): hidden_grads}
+    for i in range(1, lead + half + 1):
+        for g, ks in enumerate(plan):
+            for s in (0, 1):
+                d = i - (0 if s == 0 else lead + half - ks[-1])
+                if d == 1:
+                    begin(s, g)
+                elif 1 < d <= ks[-1]:
+                    onward(s, g, d)
+            if (i, g) in work:
+                work.pop((i, g))()
     for job in work.values():
         job()
 
@@ -266,7 +272,7 @@
     remote(inbox, inbox, psem, gsem, {"dp": dp}).wait_send()
 
 
-def on_device(chips, groups_dp, lead, at, routing, gates, hidden, w_down, dout):
+def on_device(chips, groups_dp, lead, routing, gates, hidden, w_down, dout):
     experts = 2 * chips
     cap, units = hidden.shape[3], hidden.shape[4]
     width = w_down.shape[2]
@@ -292,7 +298,7 @@
     plan, _, total = plan_of(half)
     piece = width // groups_dp
     back, grad_hidden, grad_down = pl.pallas_call(
-        functools.partial(exchange_kernel, chips, groups_dp, cap, group, lead, at),
+        functools.partial(exchange_kernel, chips, groups_dp, cap, group, lead),
         out_shape=(jax.ShapeDtypeStruct(block, BF16), jax.ShapeDtypeStruct((cap * experts, units), BF16),
                    jax.ShapeDtypeStruct((units, piece), F32)),
         in_specs=[anywhere] * 3,
@@ -300,6 +306,7 @@
         scratch_shapes=[
             pltpu.VMEM(block, BF16),
             pltpu.VMEM((cap * experts, units), BF16),
+            pltpu.VMEM((units, cap * experts), BF16),
             pltpu.VMEM((units, width), BF16),
             pltpu.VMEM(block, BF16),
             pltpu.VMEM(block, BF16),
@@ -334,8 +341,7 @@
 def solution(mesh):
     chips, groups_dp = mesh.shape["expert"] // 2, mesh.shape["dp"]
     half = chips // 2
-    lead = max(1, half - 4)
-    at = half - lead + 4
+    lead = max(1, half // 2)
     placed = (
         P(("dp", "expert"), None),
         P(("dp", "expert"), None),
@@ -344,7 +350,7 @@
         P(("dp", "expert"), None),
     )
     return jax.shard_map(
-        functools.partial(on_device, chips, groups_dp, lead, at),
+        functools.partial(on_device, chips, groups_dp, lead),
         mesh=mesh,
         in_specs=placed,
         out_specs=(

time: 338 us -> 310 us (0.917)
  the two profiles are of different devices: /device:TPU:28 before, /device:TPU:6 now
where the time goes in v2:
time: 310 us; the launch traced here: 307 us
  Pallas kernels  305 us (98%)
    pallas_call x1, Pallas kernels, on_device(): pl.pallas_call(functools.partial(exchange_kernel, chips, groups_dp, cap,...  296 us

profile of v2, /device:TPU:6, one launch (start us, length us, event | category | flops | bytes accessed | tf_op | source)
XLA Modules:
  0.0 306.9 jit_solution(16957403015016915540)
XLA Ops:
  0.6 4.2 %pack.1 = (bf16[64,48,256]{2,1,0:T(8,128)(2,1)}, s32[2,128]{1,0:T(2,128)}) custom-call(s32[2,128]{1,0:T(2,128)} %bitcast.21, f32[2,128]{1,0:T(2,128)} %bitcast.19, bf16[128,2048]{1,0:T(8,128)(2,1)} %dout_ref.3), custom_call_target="tpu_custom_call" | custom-call | tf_op jit(solution)/shard_map/pack/pallas_call | solution.py:288
  4.8 295.9 %exchange.1 = (bf16[64,48,256]{2,1,0:T(8,128)(2,1)}, bf16[384,768]{1,0:T(8,128)(2,1)}, f32[768,128]{1,0:T(8,128)}) custom-call(bf16[64,48,256]{2,1,0:T(8,128)(2,1)} %get-tuple-element.11.a_ref, bf16[384,768]{1,0:T(8,128)(2,1)} %bitcast.17, bf16[768,2048]{1,0:T(8,128)(2,1)} %bitcast.15), custom_call_target="tpu_custom_call" | custom-call | tf_op jit(solution)/shard_map/exchange/pallas_call | solution.py:300
  300.8 0.0 copy-start
  300.8 0.0 copy-start.1
  300.8 4.5 %combine.1 = (bf16[128,2048]{1,0:T(8,128)(2,1)}, f32[2,128]{1,0:T(2,128)}) custom-call(bf16[64,48,256]{2,1,0:T(8,128)(2,1)} %get-tuple-element.12.blocks_ref, s32[2,128]{1,0:T(2,128)} %get-tuple-element.13.loc_ref, f32[2,128]{1,0:T(2,128)} %bitcast.20, bf16[128,2048]{1,0:T(8,128)(2,1)} %dout_ref.3), custom_call_target="tpu_custom_call" | custom-call | tf_op jit(solution)/shard_map/combine/pallas_call | solution.py:329
  305.3 0.0 copy-done
  305.3 0.8 copy.11
  306.1 0.0 copy-done.1
  306.1 0.7 copy.12
Async XLA Ops:
  300.8 4.5 %copy-start = (bf16[384,768]{1,0:T(8,128)(2,1)S(1)}, bf16[384,768]{1,0:T(8,128)(2,1)}, u32[]{:S(2)}) copy-start(bf16[384,768]{1,0:T(8,128)(2,1)} %get-tuple-element.16) | copy-start | bytes 1769476
  300.8 5.3 %copy-start.1 = (f32[768,128]{1,0:T(8,128)S(1)}, f32[768,128]{1,0:T(8,128)}, u32[]{:S(2)}) copy-start(f32[768,128]{1,0:T(8,128)} %get-tuple-element.17) | copy-start | bytes 1179652
